TPU v7x, 512 devices: a whole 4x8x8 slice. The times are simulated.
512 devices in a mesh: rows: 8 (over y), mp: 64 (over z, x, core).
Axes of the slice: x: 4, y: 8, z: 8, core: 2. Of those that a mesh axis runs over, the one named last changes fastest.
Arguments:
- lam_out: bfloat16 [1024, 64, 1024], P('mp', 'rows'), may hold values from -6 to 6
- q_down: bfloat16 [1024, 4096], P(None, 'rows'), may hold values from -127 to 127, as said below
- down_scale: float32 [1024], replicated, may hold values from 0.0001 to 0.001
- q_up: bfloat16 [4096, 1024], P('rows'), may hold values from -127 to 127, as said below
- up_scale: float32 [4096], P('rows'), may hold values from 5e-05 to 0.0005
- chan_slopes: bfloat16 [2, 1024, 8, 4096], P(None, 'mp', 'rows'), may hold values from -0.14941406 to 1.09375
- chan_icpt: bfloat16 [2, 1024, 8, 4096], P(None, 'mp', 'rows')
- tok_in_blocks: bfloat16 [16, 128, 128], replicated, may hold values from -0.25 to 0.25
- tok_out_blocks: bfloat16 [16, 128, 128], replicated, may hold values from -0.25 to 0.25
- block_cells: int32 [16], replicated, may hold values from 0 to 31, as said below
- tok_slopes: bfloat16 [2, 512, 8, 1024], P(None, None, 'rows', 'mp'), may hold values from -0.14941406 to 1.09375
- tok_icpt: bfloat16 [2, 512, 8, 1024], P(None, None, 'rows', 'mp')
Outputs:
- lam_in: bfloat16 [1024, 64, 1024], P(None, 'rows', 'mp')
- bias: float32 [64], P('rows')
Inputs may be any that keep to these rules, and one draw needn't show every extreme that they name: `q_down`: integer values, 8-bit signed codes; a program may carry them across devices in any exact packed form, several codes to an element. `q_up`: integer values, 8-bit signed codes; a program may carry them across devices in any exact packed form, several codes to an element. `block_cells`: 16 distinct cells; cell h * 8 + u is hidden block h and token block u.
All inputs are finite; a program needn't handle non-finite values.
Results may differ from a plain program's by a relative error of at most 0.012.
Values may be sent and summed in bfloat16 or wider, within the bound.
No kernel may reach another device: no remote copies, remote signals or barrier semaphores. Data moves between devices by JAX's collectives and lax.ppermute only.
A program may use at most 64 MiB of HBM per device.

v0:
```python
import jax
import jax.numpy as jnp
from jax import lax
from jax.sharding import PartitionSpec as P

D = 1024
CH = 4096
TH = 512
TOK = 1024
BLK = 128
SPEC = 8
IMG_DEV = 1
NHB = 4
NTB = 8


def dense_blocks(blocks, cells, count_rows, count_cols):
    row_hot = (
        cells[:, None] // count_cols == jnp.arange(count_rows, dtype=jnp.int32)[None, :]
    ).astype(jnp.float32)
    col_hot = (
        cells[:, None] % count_cols == jnp.arange(count_cols, dtype=jnp.int32)[None, :]
    ).astype(jnp.float32)
    dense = jnp.einsum("bh,bt,bij->hitj", row_hot, col_hot, blocks.astype(jnp.float32))
    return dense.reshape(count_rows * BLK, count_cols * BLK).astype(jnp.bfloat16)


def relax(pre, slopes, icpt):
    pos = jnp.maximum(pre, 0.0)
    neg = jnp.minimum(pre, 0.0)
    lower = slopes[0].astype(jnp.float32)[:, :, None, :]
    upper = slopes[1].astype(jnp.float32)[:, :, None, :]
    icpt_low = icpt[0].astype(jnp.float32)[:, :, None, :]
    icpt_high = icpt[1].astype(jnp.float32)[:, :, None, :]
    mid = pos * lower + neg * upper
    row_bias = jnp.sum(pos * icpt_low + neg * icpt_high, axis=(0, 3)).reshape(-1)
    return (mid, row_bias)


def on_device(
    lam_out,
    q_down,
    down_scale,
    q_up,
    up_scale,
    chan_slopes,
    chan_icpt,
    tok_in_blocks,
    tok_out_blocks,
    block_cells,
    tok_slopes,
    tok_icpt,
):
    tok_dev = lam_out.shape[0]
    rows_dev = lam_out.shape[1]
    rows_all = rows_dev * lax.axis_size("rows")
    offset = lax.axis_index("rows") * rows_dev
    scaled = (lam_out.astype(jnp.float32) * down_scale).astype(jnp.bfloat16)
    flat = scaled.reshape(-1, D)
    pre = jnp.dot(
        flat, lax.all_gather(q_down, "rows", axis=1, tiled=True), preferred_element_type=jnp.float32
    )
    pre = pre.reshape(tok_dev, IMG_DEV, SPEC, CH)
    mid, own_bias = relax(pre, chan_slopes, chan_icpt)
    mid_flat = mid.reshape(-1, CH)
    codes = lax.all_gather(q_up, "rows", axis=0, tiled=True)
    scales = lax.all_gather(up_scale.astype(jnp.bfloat16), "rows", axis=0, tiled=True).astype(
        jnp.float32
    )
    weighted = (mid_flat * scales).astype(jnp.bfloat16)
    summed = jnp.dot(weighted, codes, preferred_element_type=jnp.float32)
    summed = summed.reshape(tok_dev, rows_dev, D)
    chan_bias = lax.dynamic_update_slice_in_dim(
        jnp.zeros((rows_all,), jnp.float32), own_bias, offset, 0
    )
    lam_res = (lam_out.astype(jnp.float32) + summed).astype(jnp.bfloat16)
    turned = lax.all_to_all(lam_res, "mp", split_axis=2, concat_axis=0, tiled=True)
    chan_dev = turned.shape[2]
    columns = turned.reshape(TOK, rows_dev * chan_dev)
    tok_in = dense_blocks(tok_in_blocks, block_cells, NHB, NTB)
    swapped = block_cells % NTB * NHB + block_cells // NTB
    tok_out = dense_blocks(tok_out_blocks, swapped, NTB, NHB)
    tpre = lax.dot_general(
        tok_out, columns, (((0,), (0,)), ((), ())), preferred_element_type=jnp.float32
    )
    tpre = tpre.reshape(TH, IMG_DEV, SPEC, chan_dev)
    tmid, tok_bias = relax(tpre, tok_slopes, tok_icpt)
    tmid = tmid.astype(jnp.bfloat16).reshape(TH, rows_dev * chan_dev)
    back = lax.dot_general(
        tok_in, tmid, (((0,), (0,)), ((), ())), preferred_element_type=jnp.float32
    )
    lam_in = (turned.astype(jnp.float32) + back.reshape(TOK, rows_dev, chan_dev)).astype(
        jnp.bfloat16
    )
    placed = lax.dynamic_update_slice_in_dim(
        jnp.zeros((rows_all,), jnp.float32), tok_bias, offset, 0
    )
    totals = lax.psum(chan_bias + placed, ("rows", "mp"))
    bias = lax.dynamic_slice_in_dim(totals, offset, rows_dev, 0)
    return (lam_in, bias)


def solution(mesh):
    return jax.shard_map(
        on_device,
        mesh=mesh,
        in_specs=(
            P("mp", "rows", None),
            P(None, "rows"),
            P(),
            P("rows", None),
            P("rows"),
            P(None, "mp", "rows", None),
            P(None, "mp", "rows", None),
            P(),
            P(),
            P(),
            P(None, None, "rows", "mp"),
            P(None, None, "rows", "mp"),
        ),
        out_specs=(P(None, "rows", "mp"), P("rows")),
        check_vma=False,
    )
```

profile of v0, /device:TPU:1, one launch (start us, length us, event | category | flops | bytes accessed | tf_op | source)
XLA Modules:
  0.0 366.1 jit_solution(10095562536390558608)
XLA Ops:
  7.3 0.7 all-gather.4.cloned.1.call-update
  8.0 0.7 all-gather.6.cloned.1.call-update
  8.8 19.1 %all-gather = bf16[8,1,512]{2,1,0:T(2,128)(2,1)S(1)} all-gather(bf16[1,1,512]{2,1,0:T(2,128)(2,1)S(1)} %reshape.231), channel_id=1, replica_groups=mesh['rows'=8,'mp'=64] {'rows'}, dimensions={0}, use_global_device_ids=true | all-gather | bytes 9216 | tf_op jit(solution)/shard_map/all_gather | solution.py:67
  28.0 1.4 fusion.8
  29.5 82.6 %all-gather.4.cloned.1.call-done = bf16[1024,4096]{1,0:T(8,128)(2,1)} async-done(((bf16[1024,512]{1,0:T(8,128)(2,1)}), bf16[1024,4096]{1,0:T(8,128)(2,1)}) %all-gather.4.cloned.1.call-update) | async-done | bytes 8388624 | tf_op jit(solution)/shard_map/all_gather | solution.py:61
  112.1 5.1 %fusion.3 = (f32[128]{0:T(128)S(1)}, f32[128,4096]{1,0:T(8,128)S(1)}) fusion(f32[16,4096]{1,0:T(8,128)S(1)} %get-tuple-element.9, f32[16,4096]{1,0:T(8,128)S(1)} %get-tuple-element.8, bf16[1024,4096]{1,0:T(8,128)(2,1)} %all-gather.4.cloned.1.call-done, bf16[16,8,1024]{2,1,0:T(8,128)(2,1)S(1)} %copy-done.1, f32[1024]{0:T(1024)S(1)} %copy-done.8), kind=kOutput, calls=%fused_computation.4 | convolution fusion | flops 1077280640 | bytes 11276800 | tf_op jit(solution)/shard_map/dot_general | solution.py:60
  117.2 92.5 %all-gather.6.cloned.1.call-done = bf16[4096,1024]{1,0:T(8,128)(2,1)} async-done(((bf16[512,1024]{1,0:T(8,128)(2,1)}), bf16[4096,1024]{1,0:T(8,128)(2,1)}) %all-gather.6.cloned.1.call-update) | async-done | bytes 8388624 | tf_op jit(solution)/shard_map/all_gather | solution.py:66
  209.7 4.8 %fusion.12 = bf16[16,8,1024]{2,1,0:T(8,128)(2,1)S(1)} fusion(bf16[4096,1024]{1,0:T(8,128)(2,1)} %all-gather.6.cloned.1.call-done, f32[128,4096]{1,0:T(8,128)S(1)} %get-tuple-element.17, f32[4096]{0:T(1024)S(1)} %bitcast.143, f32[16,4096]{1,0:T(8,128)S(1)} %get-tuple-element.11, f32[16,4096]{1,0:T(8,128)S(1)} %get-tuple-element.10, ...), kind=kOutput, calls=%fused_computation.17 | convolution fusion | flops 1077805056 | bytes 11550720 | tf_op jit(solution)/shard_map/dot_general | solution.py:71
  214.6 1.7 copy.36
  216.3 2.9 reshape.241
  219.2 11.2 %all-to-all-start = ((bf16[64,2,1024]{2,1,0:T(2,128)(2,1)}), bf16[64,2,1024]{2,1,0:T(2,128)(2,1)S(1)}, u32[]{:S(2)}, u32[]{:S(2)}) async-start(bf16[64,2,1024]{2,1,0:T(2,128)(2,1)} %reshape.241), calls=%async_computation | async-start | bytes 524288 | tf_op jit(solution)/shard_map/all_to_all | solution.py:77
  230.4 2.0 copy.42
  232.4 0.5 fusion.7
  232.9 1.3 reshape.239
  234.1 0.7 bitcast_convert_fusion.6
  234.8 0.1 reduce_sum.24
  234.9 0.2 dynamic_update_slice.8
  235.2 8.4 %all-to-all-done = bf16[64,2,1024]{2,1,0:T(2,128)(2,1)S(1)} async-done(((bf16[64,2,1024]{2,1,0:T(2,128)(2,1)}), bf16[64,2,1024]{2,1,0:T(2,128)(2,1)S(1)}, u32[]{:S(2)}, u32[]{:S(2)}) %all-to-all-start) | async-done | bytes 262176 | tf_op jit(solution)/shard_map/all_to_all | solution.py:77
  243.5 1.4 reshape.242
  245.0 3.4 copy.43
  248.4 3.0 reshape.221
  251.4 1.4 fusion.34
  252.8 0.1 reduce_sum.36
  252.9 0.1 reduce_sum.37
  253.0 0.2 add_dynamic-update-slice_fusion
  253.2 94.2 %psum.7 = f32[64]{0:T(128)S(1)} all-reduce(f32[64]{0:T(128)S(1)} %add_dynamic-update-slice_fusion), channel_id=1, replica_groups=mesh['rows'=8,'mp'=64] {'rows','mp'}, use_global_device_ids=true, to_apply=%region_4.5 | all-reduce | flops 64 | bytes 512 | tf_op jit(solution)/shard_map/psum | solution.py:98
  347.4 0.6 dynamic_slice.3
  348.0 2.6 copy.38
  350.6 0.1 bitcast_convert_fusion
  350.7 2.7 copy.39
  353.4 4.8 %reshape.224 = f32[1024,8,16]{0,2,1:T(8,128)S(1)} reshape(f32[64,16,8,16]{1,0,3,2:T(8,128)} %copy.39) | data formatting | bytes 1048576 | tf_op jit(solution)/shard_map/convert_element_type | solution.py:92
  358.2 1.0 fusion.15
  (36 shorter events, 0.3 us)
Async XLA Ops:
  7.2 1.6 copy-start.9
  7.2 20.7 %copy-start.10 = (s32[16]{0:T(128)S(1)}, s32[16]{0:T(128)}, u32[]{:S(2)}) copy-start(s32[16]{0:T(128)} %param.21) | copy-start | bytes 196
  7.2 20.8 %copy-start.2 = (bf16[16,128,128]{2,1,0:T(8,128)(2,1)S(1)}, bf16[16,128,128]{2,1,0:T(8,128)(2,1)}, u32[]{:S(2)}) copy-start(bf16[16,128,128]{2,1,0:T(8,128)(2,1)} %param.20) | copy-start | bytes 1572868
  7.2 22.2 %copy-start.4 = (bf16[2,16,1,4096]{3,1,2,0:T(8,128)(2,1)S(1)}, bf16[2,16,1,4096]{3,1,2,0:T(8,128)(2,1)}, u32[]{:S(2)}) copy-start(bf16[2,16,1,4096]{3,1,2,0:T(8,128)(2,1)} %param.18) | copy-start | bytes 786436
  7.2 22.2 %copy-start.5 = (bf16[2,16,1,4096]{3,1,2,0:T(8,128)(2,1)S(1)}, bf16[2,16,1,4096]{3,1,2,0:T(8,128)(2,1)}, u32[]{:S(2)}) copy-start(bf16[2,16,1,4096]{3,1,2,0:T(8,128)(2,1)} %param.17) | copy-start | bytes 786436
  7.2 104.9 %all-gather.4.cloned.1.call-start = ((), (), s32[]{:S(2)}) async-start(), calls=%async_computation.1 | async-start | bytes 9437184 | tf_op jit(solution)/shard_map/all_gather | solution.py:61
  8.0 104.2 %copy-start.1 = (bf16[16,8,1024]{2,1,0:T(8,128)(2,1)S(1)}, bf16[16,8,1024]{2,1,0:T(8,128)(2,1)}, u32[]{:S(2)}) copy-start(bf16[16,8,1024]{2,1,0:T(8,128)(2,1)} %param.12) | copy-start | bytes 786436
  8.0 104.1 %copy-start.8 = (f32[1024]{0:T(1024)S(1)}, f32[1024]{0:T(1024)}, u32[]{:S(2)}) copy-start(f32[1024]{0:T(1024)} %param.14) | copy-start | bytes 12292
  8.0 201.8 %all-gather.6.cloned.1.call-start = ((), (), s32[]{:S(2)}) async-start(), calls=%async_computation.2 | async-start | bytes 9437184 | tf_op jit(solution)/shard_map/all_gather | solution.py:66
  219.2 13.2 %copy-start.3 = (bf16[16,128,128]{2,1,0:T(8,128)(2,1)S(1)}, bf16[16,128,128]{2,1,0:T(8,128)(2,1)}, u32[]{:S(2)}) copy-start(bf16[16,128,128]{2,1,0:T(8,128)(2,1)} %param.19) | copy-start | bytes 1572868
  219.2 24.3 %all-to-all-start = ((bf16[64,2,1024]{2,1,0:T(2,128)(2,1)}), bf16[64,2,1024]{2,1,0:T(2,128)(2,1)S(1)}, u32[]{:S(2)}, u32[]{:S(2)}) async-start(bf16[64,2,1024]{2,1,0:T(2,128)(2,1)} %reshape.241), calls=%async_computation | async-start | bytes 524288 | tf_op jit(solution)/shard_map/all_to_all | solution.py:77
  232.3 1.8 copy-start.6
  232.4 1.8 copy-start.7
  353.4 4.8 %copy-start = (bf16[512,1024,1]{1,0,2:T(8,128)(2,1)S(1)}, bf16[512,1024,1]{1,0,2:T(8,128)(2,1)}, u32[]{:S(2)}) copy-start(bf16[512,1024,1]{1,0,2:T(8,128)(2,1)} %reshape.239) | copy-start | bytes 3145732
Sparse Core Ops, SparseCore 0:
  10.1 101.9 all-gather.3
  114.2 95.5 all-gather.5
where the time goes:
time: 367 us; the launch traced here: 366 us
  waiting for transfers between devices  185 us (50%)
  blocking collectives  113 us (31%)
  local copies, waits for them, and re-layouts  26.8 us (7%)
  matrix products  14.3 us (4%)
  between operations  14.3 us (4%)
  starting transfers between devices  11.2 us (3%)
    psum x1, blocking collectives, on_device(): totals = lax.psum(chan_bias + placed, ('rows', 'mp'))  94.2 us
    all_gather x1, waiting for transfers between devices, on_device(): codes = lax.all_gather(q_up, 'rows', axis=0, tiled=True)  92.5 us
    all_gather x1, waiting for transfers between devices, on_device(): lax.all_gather(q_down, 'rows', axis=1, tiled=True)  82.6 us
    all_gather x1, blocking collectives, on_device(): lax.all_gather(up_scale.astype(jnp.bfloat16), 'rows', axis=0, tiled=True)  19.1 us
    all_to_all x1, starting transfers between devices, on_device(): lax.all_to_all(lam_res, 'mp', split_axis=2, concat_axis=0, tiled=True)  11.2 us
    all_to_all x1, waiting for transfers between devices, on_device(): lax.all_to_all(lam_res, 'mp', split_axis=2, concat_axis=0, tiled=True)  8.38 us
    convert_element_type x2, local copies, waits for them, and re-layouts, on_device(): turned.astype(jnp.float32) + back.reshape(TOK, rows_dev, chan_dev)  7.48 us
  transfers between devices with their start and end apart: 3, of which 3 were waited for; matrix products, arithmetic and copies ran while one was open for 3% of the time, Pallas kernels for 0%

commit v1 on v0

--- a/solution.py
+++ b/solution.py
@@ -95,7 +95,9 @@
     placed = lax.dynamic_update_slice_in_dim(
         jnp.zeros((rows_all,), jnp.float32), tok_bias, offset, 0
     )
-    totals = lax.psum(chan_bias + placed, ("rows", "mp"))
+    block = chan_bias + placed
+    pieces = lax.all_gather(block, ("rows", "mp"))
+    totals = jnp.sum(pieces, axis=0)
     bias = lax.dynamic_slice_in_dim(totals, offset, rows_dev, 0)
     return (lam_in, bias)
 

time: 367 us -> 333 us (0.907)
  blocking collectives: 113 us -> 78.9 us
    psum x1 -> x0, blocking collectives: 94.2 us -> none  [on_device(): totals = lax.psum(chan_bias + placed, ('rows', 'mp'))]
    all_gather x0 -> x1, blocking collectives: none -> 59.8 us  [on_device(): pieces = lax.all_gather(block, ('rows', 'mp'))]
where the time goes in v1:
time: 333 us; the launch traced here: 332 us
  waiting for transfers between devices  185 us (56%)
  blocking collectives  78.9 us (24%)
  local copies, waits for them, and re-layouts  26.9 us (8%)
  matrix products  14.3 us (4%)
  between operations  14.3 us (4%)
  starting transfers between devices  11.2 us (3%)
    all_gather x1, waiting for transfers between devices, on_device(): codes = lax.all_gather(q_up, 'rows', axis=0, tiled=True)  92.5 us
    all_gather x1, waiting for transfers between devices, on_device(): lax.all_gather(q_down, 'rows', axis=1, tiled=True)  82.6 us
    all_gather x1, blocking collectives, on_device(): pieces = lax.all_gather(block, ('rows', 'mp'))  59.8 us
    all_gather x1, blocking collectives, on_device(): lax.all_gather(up_scale.astype(jnp.bfloat16), 'rows', axis=0, tiled=True)  19.1 us
    all_to_all x1, starting transfers between devices, on_device(): lax.all_to_all(lam_res, 'mp', split_axis=2, concat_axis=0, tiled=True)  11.2 us
    all_to_all x1, waiting for transfers between devices, on_device(): lax.all_to_all(lam_res, 'mp', split_axis=2, concat_axis=0, tiled=True)  8.38 us
    convert_element_type x2, local copies, waits for them, and re-layouts, on_device(): turned.astype(jnp.float32) + back.reshape(TOK, rows_dev, chan_dev)  7.48 us
  transfers between devices with their start and end apart: 3, of which 3 were waited for; matrix products, arithmetic and copies ran while one was open for 3% of the time, Pallas kernels for 0%

profile of v1, /device:TPU:1, one launch (start us, length us, event | category | flops | bytes accessed | tf_op | source)
XLA Modules:
  0.0 332.2 jit_solution(11545687900193346057)
XLA Ops:
  7.3 0.7 all-gather.5.cloned.1.call-update
  8.0 0.7 all-gather.7.cloned.1.call-update
  8.8 19.1 %all-gather = bf16[8,1,512]{2,1,0:T(2,128)(2,1)S(1)} all-gather(bf16[1,1,512]{2,1,0:T(2,128)(2,1)S(1)} %reshape.233), channel_id=1, replica_groups=mesh['rows'=8,'mp'=64] {'rows'}, dimensions={0}, use_global_device_ids=true | all-gather | bytes 9216 | tf_op jit(solution)/shard_map/all_gather | solution.py:67
  28.0 1.4 fusion.8
  29.5 82.6 %all-gather.5.cloned.1.call-done = bf16[1024,4096]{1,0:T(8,128)(2,1)} async-done(((bf16[1024,512]{1,0:T(8,128)(2,1)}), bf16[1024,4096]{1,0:T(8,128)(2,1)}) %all-gather.5.cloned.1.call-update) | async-done | bytes 8388624 | tf_op jit(solution)/shard_map/all_gather | solution.py:61
  112.1 5.1 %fusion.3 = (f32[128]{0:T(128)S(1)}, f32[128,4096]{1,0:T(8,128)S(1)}) fusion(f32[16,4096]{1,0:T(8,128)S(1)} %get-tuple-element.9, f32[16,4096]{1,0:T(8,128)S(1)} %get-tuple-element.8, bf16[1024,4096]{1,0:T(8,128)(2,1)} %all-gather.5.cloned.1.call-done, bf16[16,8,1024]{2,1,0:T(8,128)(2,1)S(1)} %copy-done.1, f32[1024]{0:T(1024)S(1)} %copy-done.8), kind=kOutput, calls=%fused_computation.4 | convolution fusion | flops 1077280640 | bytes 11276800 | tf_op jit(solution)/shard_map/dot_general | solution.py:60
  117.2 92.5 %all-gather.7.cloned.1.call-done = bf16[4096,1024]{1,0:T(8,128)(2,1)} async-done(((bf16[512,1024]{1,0:T(8,128)(2,1)}), bf16[4096,1024]{1,0:T(8,128)(2,1)}) %all-gather.7.cloned.1.call-update) | async-done | bytes 8388624 | tf_op jit(solution)/shard_map/all_gather | solution.py:66
  209.7 4.8 %fusion.12 = bf16[16,8,1024]{2,1,0:T(8,128)(2,1)S(1)} fusion(bf16[4096,1024]{1,0:T(8,128)(2,1)} %all-gather.7.cloned.1.call-done, f32[128,4096]{1,0:T(8,128)S(1)} %get-tuple-element.17, f32[4096]{0:T(1024)S(1)} %bitcast.146, f32[16,4096]{1,0:T(8,128)S(1)} %get-tuple-element.11, f32[16,4096]{1,0:T(8,128)S(1)} %get-tuple-element.10, ...), kind=kOutput, calls=%fused_computation.17 | convolution fusion | flops 1077805056 | bytes 11550720 | tf_op jit(solution)/shard_map/dot_general | solution.py:71
  214.6 1.7 copy.36
  216.3 2.9 reshape.249
  219.2 11.2 %all-to-all-start = ((bf16[64,2,1024]{2,1,0:T(2,128)(2,1)}), bf16[64,2,1024]{2,1,0:T(2,128)(2,1)S(1)}, u32[]{:S(2)}, u32[]{:S(2)}) async-start(bf16[64,2,1024]{2,1,0:T(2,128)(2,1)} %reshape.249), calls=%async_computation | async-start | bytes 524288 | tf_op jit(solution)/shard_map/all_to_all | solution.py:77
  230.4 2.0 copy.42
  232.4 0.5 fusion.7
  232.9 1.3 reshape.247
  234.1 0.7 bitcast_convert_fusion.6
  234.9 0.2 dynamic_update_slice.8
  235.2 8.4 %all-to-all-done = bf16[64,2,1024]{2,1,0:T(2,128)(2,1)S(1)} async-done(((bf16[64,2,1024]{2,1,0:T(2,128)(2,1)}), bf16[64,2,1024]{2,1,0:T(2,128)(2,1)S(1)}, u32[]{:S(2)}, u32[]{:S(2)}) %all-to-all-start) | async-done | bytes 262176 | tf_op jit(solution)/shard_map/all_to_all | solution.py:77
  243.5 1.4 reshape.250
  245.0 3.4 %copy.43 = bf16[64,16,8,16]{3,2,1,0:T(8,128)(2,1)} copy(bf16[64,16,8,16]{1,2,3,0:T(8,128)(2,1)S(1)} %bitcast.142) | data formatting | bytes 524288 | tf_op jit(solution)/shard_map/all_to_all | solution.py:77
  248.4 3.0 reshape.223
  251.4 1.4 fusion.34
  252.9 0.1 reduce_sum.46
  253.0 0.1 add_bitcast_fusion
  253.1 0.1 add.74
  253.2 59.8 %all-gather.1 = f32[512,1,64]{2,1,0:T(1,128)S(1)} all-gather(f32[1,1,64]{2,1,0:T(1,128)S(1)} %add.74), channel_id=1, replica_groups=mesh['rows'=8,'mp'=64] {'rows','mp'}, dimensions={0}, use_global_device_ids=true | all-gather | bytes 131328 | tf_op jit(solution)/shard_map/all_gather | solution.py:99
  313.0 0.6 reduce_sum.47
  313.5 0.6 dynamic_slice.3
  314.1 2.6 copy.38
  316.7 0.1 bitcast_convert_fusion
  316.8 2.7 copy.39
  319.5 4.8 %reshape.226 = f32[1024,8,16]{0,2,1:T(8,128)S(1)} reshape(f32[64,16,8,16]{1,0,3,2:T(8,128)} %copy.39) | data formatting | bytes 1048576 | tf_op jit(solution)/shard_map/convert_element_type | solution.py:92
  324.3 1.0 fusion.15
  (38 shorter events, 0.5 us)
Async XLA Ops:
  7.2 1.6 copy-start.9
  7.2 20.7 %copy-start.10 = (s32[16]{0:T(128)S(1)}, s32[16]{0:T(128)}, u32[]{:S(2)}) copy-start(s32[16]{0:T(128)} %param.21) | copy-start | bytes 196
  7.2 20.8 %copy-start.2 = (bf16[16,128,128]{2,1,0:T(8,128)(2,1)S(1)}, bf16[16,128,128]{2,1,0:T(8,128)(2,1)}, u32[]{:S(2)}) copy-start(bf16[16,128,128]{2,1,0:T(8,128)(2,1)} %param.20) | copy-start | bytes 1572868
  7.2 22.2 %copy-start.4 = (bf16[2,16,1,4096]{3,1,2,0:T(8,128)(2,1)S(1)}, bf16[2,16,1,4096]{3,1,2,0:T(8,128)(2,1)}, u32[]{:S(2)}) copy-start(bf16[2,16,1,4096]{3,1,2,0:T(8,128)(2,1)} %param.18) | copy-start | bytes 786436
  7.2 22.2 %copy-start.5 = (bf16[2,16,1,4096]{3,1,2,0:T(8,128)(2,1)S(1)}, bf16[2,16,1,4096]{3,1,2,0:T(8,128)(2,1)}, u32[]{:S(2)}) copy-start(bf16[2,16,1,4096]{3,1,2,0:T(8,128)(2,1)} %param.17) | copy-start | bytes 786436
  7.2 104.9 %all-gather.5.cloned.1.call-start = ((), (), s32[]{:S(2)}) async-start(), calls=%async_computation.1 | async-start | bytes 9437184 | tf_op jit(solution)/shard_map/all_gather | solution.py:61
  8.0 104.2 %copy-start.1 = (bf16[16,8,1024]{2,1,0:T(8,128)(2,1)S(1)}, bf16[16,8,1024]{2,1,0:T(8,128)(2,1)}, u32[]{:S(2)}) copy-start(bf16[16,8,1024]{2,1,0:T(8,128)(2,1)} %param.12) | copy-start | bytes 786436
  8.0 104.1 %copy-start.8 = (f32[1024]{0:T(1024)S(1)}, f32[1024]{0:T(1024)}, u32[]{:S(2)}) copy-start(f32[1024]{0:T(1024)} %param.14) | copy-start | bytes 12292
  8.0 201.8 %all-gather.7.cloned.1.call-start = ((), (), s32[]{:S(2)}) async-start(), calls=%async_computation.2 | async-start | bytes 9437184 | tf_op jit(solution)/shard_map/all_gather | solution.py:66
  219.2 13.2 %copy-start.3 = (bf16[16,128,128]{2,1,0:T(8,128)(2,1)S(1)}, bf16[16,128,128]{2,1,0:T(8,128)(2,1)}, u32[]{:S(2)}) copy-start(bf16[16,128,128]{2,1,0:T(8,128)(2,1)} %param.19) | copy-start | bytes 1572868
  219.2 24.3 %all-to-all-start = ((bf16[64,2,1024]{2,1,0:T(2,128)(2,1)}), bf16[64,2,1024]{2,1,0:T(2,128)(2,1)S(1)}, u32[]{:S(2)}, u32[]{:S(2)}) async-start(bf16[64,2,1024]{2,1,0:T(2,128)(2,1)} %reshape.249), calls=%async_computation | async-start | bytes 524288 | tf_op jit(solution)/shard_map/all_to_all | solution.py:77
  232.3 1.8 copy-start.6
  232.4 1.8 copy-start.7
  319.5 4.8 %copy-start = (bf16[512,1024,1]{1,0,2:T(8,128)(2,1)S(1)}, bf16[512,1024,1]{1,0,2:T(8,128)(2,1)}, u32[]{:S(2)}) copy-start(bf16[512,1024,1]{1,0,2:T(8,128)(2,1)} %reshape.247) | copy-start | bytes 3145732
Sparse Core Ops, SparseCore 0:
  10.1 101.9 all-gather.4
  114.2 95.5 all-gather.6
